TPU v7x, 128 devices: a whole 4x4x4 slice. The times are simulated.
128 devices in a mesh: batch: 4 (over z), head: 2 (over core), seq: 16 (over x, y).
Axes of the slice: x: 4, y: 4, z: 4, core: 2. Of those that a mesh axis runs over, the one named last changes fastest.
Arguments:
- hidden: float32 [32768, 8192], P(('batch', 'seq')), parts along dimension 0, may hold values from -6 to 6
- row_scale: float32 [32768], P(('batch', 'seq')), parts along dimension 0, may hold values from 0.25 to 4
- key_value_weight: float32 [8192, 8, 256], P('seq', 'head'), may hold values from -0.0625 to 0.0625
- outlier: int32 [512, 8], P(('batch', 'seq'), 'head'), parts along dimension 0, may hold values 0 or 1
- sketch_sign_flags: int32 [8, 2, 128, 64], P('head'), may hold values from 0 to 1
Outputs:
- left: bfloat16 [8, 32768, 128], P('head', ('batch', 'seq')), parts along dimension 1
- right: float32 [32, 128, 128], P(('batch', 'head')), parts along dimension 0
There are 4 independent parts, one for each index of `batch`. A program takes and returns all parts, laid end to end along the dimension named above; an argument that names none is the same for every part. Nothing has to cross between parts.
All inputs are finite; a program needn't handle non-finite values. No bound on the sum of `outlier` on one device may be relied on, other than what follows from the above.
Results may differ from a plain program's by a relative error of at most 0.0015.
Values sent between devices are 32-bit elements; how exact they have to be, the bound alone decides.
No kernel may reach another device: no remote copies, remote signals or barrier semaphores. Data moves between devices by JAX's collectives and lax.ppermute only.
A program may use at most 192 MiB of HBM per device.

v0:
```python
import math
import jax
import jax.numpy as jnp
from jax import lax
from jax.sharding import PartitionSpec as P

ITERS = 2
complete_cycle = 2.0 * math.pi


def shards(hidden, row_scale, key_value_weight, outlier, sketch_sign_flags):
    tok_rows = hidden.shape[0]
    head_count = key_value_weight.shape[1]
    kv_cols = key_value_weight.shape[2]
    head_dim = kv_cols // 2
    rank_cols = sketch_sign_flags.shape[3]
    group_count = outlier.shape[0]
    highest = lax.Precision.HIGHEST
    weight_piece = lax.all_gather(key_value_weight, "seq", axis=0, tiled=True)
    flat_piece = weight_piece.reshape(weight_piece.shape[0], head_count * kv_cols)
    projected_key_value = jnp.dot(hidden, flat_piece, precision=highest)
    projected_key_value = projected_key_value * row_scale[:, None]
    grouped_rows = projected_key_value.reshape(
        group_count, tok_rows // group_count, head_count, kv_cols
    )
    quantization_spacing = jnp.max(jnp.abs(grouped_rows), axis=1, keepdims=True) / 7.0 + 1e-06
    retain_mask = (1 - outlier).astype(jnp.float32)[:, None, :, None]
    residual_error = (
        retain_mask * jnp.sin(complete_cycle * grouped_rows / quantization_spacing)
    ).reshape(tok_rows, head_count, 2, head_dim)
    sign_matrix = (2 * sketch_sign_flags - 1).astype(jnp.float32)
    sketch = jnp.einsum("thec,heck->thek", residual_error, sign_matrix, precision=highest)
    for iteration in range(ITERS):
        local_gram = jnp.einsum("thek,theq->hekq", sketch, sketch, precision=highest)
        gram_matrix = lax.psum(local_gram, "seq")
        lower_factor = jnp.linalg.cholesky(gram_matrix)
        identity = jnp.broadcast_to(jnp.eye(rank_cols, dtype=gram_matrix.dtype), gram_matrix.shape)
        inverse_factor = jax.scipy.linalg.solve_triangular(lower_factor, identity, lower=True)
        basis_matrix = jnp.einsum("thek,heqk->theq", sketch, inverse_factor, precision=highest)
        local_coef = jnp.einsum("thec,theq->hecq", residual_error, basis_matrix, precision=highest)
        coefficient_rows = lax.psum(local_coef, "seq")
        if iteration + 1 < ITERS:
            sketch = jnp.einsum(
                "thec,hecq->theq", residual_error, coefficient_rows, precision=highest
            )
    root_length = math.sqrt(tok_rows * lax.axis_size("seq"))
    left = (
        (root_length * basis_matrix)
        .transpose(1, 0, 2, 3)
        .reshape(head_count, tok_rows, 2 * rank_cols)
        .astype(jnp.bfloat16)
    )
    right = (
        (coefficient_rows / root_length)
        .transpose(0, 2, 1, 3)
        .reshape(head_count, head_dim, 2 * rank_cols)
    )
    return (left, right)


def solution(mesh):
    return jax.shard_map(
        shards,
        mesh=mesh,
        in_specs=(
            P(("batch", "seq"), None),
            P(("batch", "seq")),
            P("seq", "head", None),
            P(("batch", "seq"), "head"),
            P("head", None, None, None),
        ),
        out_specs=(P("head", ("batch", "seq"), None), P(("batch", "head"), None, None)),
        check_vma=False,
    )
```

profile of v0, /device:TPU:0, one launch (start us, length us, event | category | flops | bytes accessed | tf_op | source)
XLA Modules:
  0.0 858.8 jit_solution(14637617141155702260)
XLA Ops:
  8.1 201.4 %all-gather.2.cloned.1.call-done = f32[8192,4,256]{2,1,0:T(4,128)} async-done(((f32[512,4,256]{2,1,0:T(4,128)}), f32[8192,4,256]{2,1,0:T(4,128)}) %all-gather.2.cloned.1.call-update) | async-done | bytes 33554448 | tf_op jit(solution)/shard_map/all_gather | solution.py:19
  209.6 27.5 %copy.108 = f32[1024,8,4,256]{3,1,2,0:T(8,128)} copy(f32[1024,8,4,256]{3,2,1,0:T(4,128)} %bitcast.58) | data formatting | bytes 67108864
  237.1 60.5 %multiply_abs_fusion = (f32[512,1024]{1,0:T(8,128)}, f32[512,1024]{1,0:T(8,128)}) fusion(f32[512]{0:T(512)S(1)} %copy-done.3, f32[512,8192]{1,0:T(8,128)} %param.8, f32[8192,1024]{1,0:T(8,128)} %bitcast.59), kind=kOutput, calls=%fused_computation.3 | convolution fusion | flops 51541180416 | bytes 54528000 | tf_op jit(solution)/shard_map/dot_general | solution.py:21
  297.6 2.2 abs.7
  300.3 2.1 div.32
  302.4 1.9 copy.86
  304.4 1.8 copy.88
  306.2 8.9 %fusion.1 = f32[512,4,2,128]{3,0,2,1:T(8,128)S(1)} fusion(f32[512,4,2,128]{3,0,2,1:T(8,128)} %copy.88, f32[512,4,2,128]{3,2,0,1:T(2,128)} %div.32, f32[512,4]{0,1:T(4,128)S(1)} %mul.46), kind=kLoop, calls=%fused_computation.2 | loop fusion | flops 1048576 | bytes 6299648 | tf_op jit(solution)/shard_map/mul | solution.py:29
  315.1 2.4 convolution_bitcast_fusion.1
  317.5 1.8 fusion.21
  319.4 83.9 %all-reduce.5.cloned.1.call-done = f32[4,2,64,64]{2,3,1,0:T(8,128)} async-done(((f32[4,2,64,64]{2,3,1,0:T(8,128)}), f32[4,2,64,64]{2,3,1,0:T(8,128)}) %all-reduce.5.cloned.1.call-update) | async-done | bytes 131088 | tf_op jit(solution)/shard_map/psum | solution.py:35
  403.3 1.1 copy.91
  404.3 1.7 fusion.9
  406.0 47.6 %custom-call.8 = f32[4,2,64,64]{3,2,1,0:T(8,128)S(1)} custom-call(f32[4,2,64,64]{3,2,1,0:T(8,128)} %fusion.9), custom_call_target="Cholesky" | custom-call | tf_op jit(solution)/shard_map/jit(cholesky)/cholesky | solution.py:36
  453.8 0.8 select_bitcast_fusion.1
  454.7 40.0 %custom-call.9 = f32[4,2,1,64,64]{3,4,2,1,0:T(8,128)S(1)} custom-call(f32[4,2,1,64,64]{4,3,2,1,0:T(8,128)} %select_bitcast_fusion.1), custom_call_target="InvertDiagBlocksLowerTriangular" | custom-call | tf_op jit(solution)/shard_map/jit(_solve_triangular)/vmap(vmap())/triangular_solve | solution.py:38
  495.3 1.0 convolution_bitcast_fusion.2
  496.3 2.2 fusion.22
  498.6 83.5 %all-reduce.7.cloned.1.call-done = f32[4,2,128,64]{2,3,1,0:T(8,128)} async-done(((f32[4,2,128,64]{2,3,1,0:T(8,128)}), f32[4,2,128,64]{2,3,1,0:T(8,128)}) %all-reduce.7.cloned.1.call-update) | async-done | bytes 262160 | tf_op jit(solution)/shard_map/psum | solution.py:41
  582.1 3.3 convolution_bitcast_fusion
  585.4 1.8 fusion.23
  587.3 83.6 %all-reduce.9.cloned.1.call-done = f32[4,2,64,64]{2,3,1,0:T(8,128)} async-done(((f32[4,2,64,64]{2,3,1,0:T(8,128)}), f32[4,2,64,64]{2,3,1,0:T(8,128)}) %all-reduce.9.cloned.1.call-update) | async-done | bytes 131088 | tf_op jit(solution)/shard_map/psum | solution.py:35
  670.8 1.1 copy.96
  671.9 1.7 fusion.6
  673.6 47.6 %custom-call.10 = f32[4,2,64,64]{3,2,1,0:T(8,128)S(1)} custom-call(f32[4,2,64,64]{3,2,1,0:T(8,128)} %fusion.6), custom_call_target="Cholesky" | custom-call | tf_op jit(solution)/shard_map/jit(cholesky)/cholesky | solution.py:36
  722.2 40.0 %custom-call.11 = f32[4,2,1,64,64]{3,4,2,1,0:T(8,128)S(1)} custom-call(f32[4,2,1,64,64]{4,3,2,1,0:T(8,128)} %select_bitcast_fusion), custom_call_target="InvertDiagBlocksLowerTriangular" | custom-call | tf_op jit(solution)/shard_map/jit(_solve_triangular)/vmap(vmap())/triangular_solve | solution.py:38
  762.9 1.8 multiply_convert_fusion
  764.7 2.2 fusion.2
  766.9 1.0 copy.100
  767.9 82.5 %all-reduce.11.cloned.1.call-done = f32[4,2,128,64]{2,3,1,0:T(8,128)} async-done(((f32[4,2,128,64]{2,3,1,0:T(8,128)}), f32[4,2,128,64]{2,3,1,0:T(8,128)}) %all-reduce.11.cloned.1.call-update) | async-done | bytes 262160 | tf_op jit(solution)/shard_map/psum | solution.py:41
  850.5 1.0 broadcast_multiply_fusion
  851.4 0.8 copy.101
  (34 shorter events, 4.0 us)
Async XLA Ops:
  7.2 0.8 copy-start.2
  7.2 202.4 %all-gather.2.cloned.1.call-start = ((), (), s32[]{:S(2)}) async-start(), calls=%async_computation | async-start | bytes 35651584 | tf_op jit(solution)/shard_map/all_gather | solution.py:19
  7.9 395.4 %all-reduce.5.cloned.1.call-start = ((), (), s32[]{:S(2)}) async-start(), calls=%async_computation.1 | async-start | bytes 524288 | tf_op jit(solution)/shard_map/psum | solution.py:35
  209.6 27.5 %copy-start.3 = (f32[512]{0:T(512)S(1)}, f32[512]{0:T(512)}, u32[]{:S(2)}) copy-start(f32[512]{0:T(512)} %param.9) | copy-start | bytes 6148
  306.2 8.9 %copy-start.1 = (s32[4,2,128,64]{2,3,1,0:T(8,128)S(1)}, s32[4,2,128,64]{2,3,1,0:T(8,128)}, u32[]{:S(2)}) copy-start(s32[4,2,128,64]{2,3,1,0:T(8,128)} %param.12) | copy-start | bytes 786436
  319.3 262.8 %all-reduce.7.cloned.1.call-start = ((), (), s32[]{:S(2)}) async-start(), calls=%async_computation.2 | async-start | bytes 524288 | tf_op jit(solution)/shard_map/psum | solution.py:41
  498.6 172.3 %all-reduce.9.cloned.1.call-start = ((), (), s32[]{:S(2)}) async-start(), calls=%async_computation.3 | async-start | bytes 524288 | tf_op jit(solution)/shard_map/psum | solution.py:35
  587.2 263.2 %all-reduce.11.cloned.1.call-start = ((), (), s32[]{:S(2)}) async-start(), calls=%async_computation.4 | async-start | bytes 524288 | tf_op jit(solution)/shard_map/psum | solution.py:41
  764.7 2.3 copy-start
Sparse Core Ops, SparseCore 0:
  10.1 199.3 all-gather.1
  319.4 83.7 all-reduce.4
  498.7 83.3 all-reduce.6
  587.3 83.4 all-reduce.8
  767.1 83.3 all-reduce.10
where the time goes:
time: 860 us; the launch traced here: 859 us
  waiting for transfers between devices  536 us (62%)
  other arithmetic  191 us (22%)
  matrix products  78.2 us (9%)
  local copies, waits for them, and re-layouts  39.9 us (5%)
  between operations  14 us (2%)
    all_gather x1, waiting for transfers between devices, shards(): weight_piece = lax.all_gather(key_value_weight, 'seq', axis=0, tiled=True)  201 us
    psum x2, waiting for transfers between devices, shards(): gram_matrix = lax.psum(local_gram, 'seq')  167 us
    psum x2, waiting for transfers between devices, shards(): coefficient_rows = lax.psum(local_coef, 'seq')  166 us
    another operation x7, other arithmetic, shards(): lower_factor = jnp.linalg.cholesky(gram_matrix)  95.6 us
    another operation x5, other arithmetic, shards(): jax.scipy.linalg.solve_triangular(lower_factor, identity, lower=True)  81.7 us
    dot_general x1, matrix products, shards(): projected_key_value = jnp.dot(hidden, flat_piece, precision=highest)  60.5 us
    unnamed x11, local copies, waits for them, and re-layouts  29.4 us
  transfers between devices with their start and end apart: 5, of which 5 were waited for; matrix products, arithmetic and copies ran while one was open for 0% of the time, Pallas kernels for 0%

commit v1 on v0

--- a/solution.py
+++ b/solution.py
@@ -32,7 +32,7 @@
     sketch = jnp.einsum("thec,heck->thek", residual_error, sign_matrix, precision=highest)
     for iteration in range(ITERS):
         local_gram = jnp.einsum("thek,theq->hekq", sketch, sketch, precision=highest)
-        gram_matrix = lax.psum(local_gram, "seq")
+        gram_matrix = jnp.sum(lax.all_gather(local_gram, "seq"), axis=0)
         lower_factor = jnp.linalg.cholesky(gram_matrix)
         identity = jnp.broadcast_to(jnp.eye(rank_cols, dtype=gram_matrix.dtype), gram_matrix.shape)
         inverse_factor = jax.scipy.linalg.solve_triangular(lower_factor, identity, lower=True)

time: 860 us -> 800 us (0.930)
  waiting for transfers between devices: 536 us -> 471 us
    psum x2 -> x0, waiting for transfers between devices: 167 us -> none  [shards(): gram_matrix = lax.psum(local_gram, 'seq')]
    all_gather x0 -> x2, waiting for transfers between devices: none -> 102 us  [shards(): gram_matrix = jnp.sum(lax.all_gather(local_gram, 'seq'), axis=0)]
where the time goes in v1:
time: 800 us; the launch traced here: 799 us
  waiting for transfers between devices  471 us (59%)
  other arithmetic  196 us (24%)
  matrix products  78.2 us (10%)
  local copies, waits for them, and re-layouts  39.5 us (5%)
  between operations  14 us (2%)
    all_gather x1, waiting for transfers between devices, shards(): weight_piece = lax.all_gather(key_value_weight, 'seq', axis=0, tiled=True)  201 us
    psum x2, waiting for transfers between devices, shards(): coefficient_rows = lax.psum(local_coef, 'seq')  167 us
    all_gather x2, waiting for transfers between devices, shards(): gram_matrix = jnp.sum(lax.all_gather(local_gram, 'seq'), axis=0)  102 us
    another operation x7, other arithmetic, shards(): lower_factor = jnp.linalg.cholesky(gram_matrix)  95.6 us
    another operation x5, other arithmetic, shards(): jax.scipy.linalg.solve_triangular(lower_factor, identity, lower=True)  81.7 us
    dot_general x1, matrix products, shards(): projected_key_value = jnp.dot(hidden, flat_piece, precision=highest)  60.5 us
    unnamed x11, local copies, waits for them, and re-layouts  29.4 us
  transfers between devices with their start and end apart: 5, of which 5 were waited for; matrix products, arithmetic and copies ran while one was open for 0% of the time, Pallas kernels for 0%

profile of v1, /device:TPU:0, one launch (start us, length us, event | category | flops | bytes accessed | tf_op | source)
XLA Modules:
  0.0 799.1 jit_solution(13762391619325089990)
XLA Ops:
  8.1 201.5 %all-gather.6.cloned.1.call-done = f32[8192,4,256]{2,1,0:T(4,128)} async-done(((f32[512,4,256]{2,1,0:T(4,128)}), f32[8192,4,256]{2,1,0:T(4,128)}) %all-gather.6.cloned.1.call-update) | async-done | bytes 33554448 | tf_op jit(solution)/shard_map/all_gather | solution.py:19
  209.6 27.5 %copy.92 = f32[1024,8,4,256]{3,1,2,0:T(8,128)} copy(f32[1024,8,4,256]{3,2,1,0:T(4,128)} %bitcast.60) | data formatting | bytes 67108864
  237.1 60.5 %multiply_abs_fusion = (f32[512,1024]{1,0:T(8,128)}, f32[512,1024]{1,0:T(8,128)}) fusion(f32[512]{0:T(512)S(1)} %copy-done.3, f32[512,8192]{1,0:T(8,128)} %param.8, f32[8192,1024]{1,0:T(8,128)} %bitcast.61), kind=kOutput, calls=%fused_computation.3 | convolution fusion | flops 51541180416 | bytes 54528000 | tf_op jit(solution)/shard_map/dot_general | solution.py:21
  297.6 2.2 abs.7
  300.3 2.1 div.32
  302.4 1.9 copy.74
  304.4 1.8 copy.76
  306.2 8.9 %fusion.1 = f32[512,4,2,128]{3,0,2,1:T(8,128)S(1)} fusion(f32[512,4,2,128]{3,0,2,1:T(8,128)} %copy.76, f32[512,4,2,128]{3,2,0,1:T(2,128)} %div.32, f32[512,4]{0,1:T(4,128)S(1)} %mul.46), kind=kLoop, calls=%fused_computation.2 | loop fusion | flops 1048576 | bytes 6299648 | tf_op jit(solution)/shard_map/mul | solution.py:29
  315.1 2.4 convolution_bitcast_fusion.1
  317.5 1.8 fusion.21
  319.4 51.2 %all-gather.8.cloned.1.call-done = f32[64,2,64,64]{3,2,1,0:T(8,128)} async-done(((f32[4,2,64,64]{3,2,1,0:T(8,128)}), f32[64,2,64,64]{3,2,1,0:T(8,128)}) %all-gather.8.cloned.1.call-update) | async-done | bytes 2097168 | tf_op jit(solution)/shard_map/all_gather | solution.py:35
  370.6 2.7 reduce_sum.18
  373.3 0.8 copy.78
  374.1 1.7 fusion.9
  375.8 47.6 %custom-call.8 = f32[4,2,64,64]{3,2,1,0:T(8,128)S(1)} custom-call(f32[4,2,64,64]{3,2,1,0:T(8,128)} %fusion.9), custom_call_target="Cholesky" | custom-call | tf_op jit(solution)/shard_map/jit(cholesky)/cholesky | solution.py:36
  424.5 40.0 %custom-call.9 = f32[4,2,1,64,64]{3,4,2,1,0:T(8,128)S(1)} custom-call(f32[4,2,1,64,64]{4,3,2,1,0:T(8,128)} %select_bitcast_fusion.1), custom_call_target="InvertDiagBlocksLowerTriangular" | custom-call | tf_op jit(solution)/shard_map/jit(_solve_triangular)/vmap(vmap())/triangular_solve | solution.py:38
  465.1 1.0 convolution_bitcast_fusion.2
  466.1 2.2 fusion.22
  468.4 83.8 %all-reduce.3.cloned.1.call-done = f32[4,2,128,64]{2,3,1,0:T(8,128)} async-done(((f32[4,2,128,64]{2,3,1,0:T(8,128)}), f32[4,2,128,64]{2,3,1,0:T(8,128)}) %all-reduce.3.cloned.1.call-update) | async-done | bytes 262160 | tf_op jit(solution)/shard_map/psum | solution.py:41
  552.2 3.3 convolution_bitcast_fusion
  555.6 1.8 fusion.23
  557.7 50.7 %all-gather.10.cloned.1.call-done = f32[64,2,64,64]{3,2,1,0:T(8,128)} async-done(((f32[4,2,64,64]{3,2,1,0:T(8,128)}), f32[64,2,64,64]{3,2,1,0:T(8,128)}) %all-gather.10.cloned.1.call-update) | async-done | bytes 2097168 | tf_op jit(solution)/shard_map/all_gather | solution.py:35
  608.4 2.7 reduce_sum.19
  611.0 0.8 copy.82
  611.9 1.7 fusion.6
  613.6 47.6 %custom-call.10 = f32[4,2,64,64]{3,2,1,0:T(8,128)S(1)} custom-call(f32[4,2,64,64]{3,2,1,0:T(8,128)} %fusion.6), custom_call_target="Cholesky" | custom-call | tf_op jit(solution)/shard_map/jit(cholesky)/cholesky | solution.py:36
  662.2 40.0 %custom-call.11 = f32[4,2,1,64,64]{3,4,2,1,0:T(8,128)S(1)} custom-call(f32[4,2,1,64,64]{4,3,2,1,0:T(8,128)} %select_bitcast_fusion), custom_call_target="InvertDiagBlocksLowerTriangular" | custom-call | tf_op jit(solution)/shard_map/jit(_solve_triangular)/vmap(vmap())/triangular_solve | solution.py:38
  702.9 1.8 multiply_convert_fusion
  704.6 2.2 fusion.2
  706.9 1.0 copy.86
  707.9 82.9 %all-reduce.5.cloned.1.call-done = f32[4,2,128,64]{2,3,1,0:T(8,128)} async-done(((f32[4,2,128,64]{2,3,1,0:T(8,128)}), f32[4,2,128,64]{2,3,1,0:T(8,128)}) %all-reduce.5.cloned.1.call-update) | async-done | bytes 262160 | tf_op jit(solution)/shard_map/psum | solution.py:41
  790.8 1.0 broadcast_multiply_fusion
  (36 shorter events, 5.9 us)
Async XLA Ops:
  7.2 0.8 copy-start.2
  7.2 202.4 %all-gather.6.cloned.1.call-start = ((), (), s32[]{:S(2)}) async-start(), calls=%async_computation | async-start | bytes 35651584 | tf_op jit(solution)/shard_map/all_gather | solution.py:19
  7.9 362.7 %all-gather.8.cloned.1.call-start = ((), (), s32[]{:S(2)}) async-start(), calls=%async_computation.3 | async-start | bytes 4456448 | tf_op jit(solution)/shard_map/all_gather | solution.py:35
  209.6 27.5 %copy-start.3 = (f32[512]{0:T(512)S(1)}, f32[512]{0:T(512)}, u32[]{:S(2)}) copy-start(f32[512]{0:T(512)} %param.9) | copy-start | bytes 6148
  306.2 8.9 %copy-start.1 = (s32[4,2,128,64]{2,3,1,0:T(8,128)S(1)}, s32[4,2,128,64]{2,3,1,0:T(8,128)}, u32[]{:S(2)}) copy-start(s32[4,2,128,64]{2,3,1,0:T(8,128)} %param.12) | copy-start | bytes 786436
  319.3 232.9 %all-reduce.3.cloned.1.call-start = ((), (), s32[]{:S(2)}) async-start(), calls=%async_computation.1 | async-start | bytes 524288 | tf_op jit(solution)/shard_map/psum | solution.py:41
  468.4 140.0 %all-gather.10.cloned.1.call-start = ((), (), s32[]{:S(2)}) async-start(), calls=%async_computation.4 | async-start | bytes 4456448 | tf_op jit(solution)/shard_map/all_gather | solution.py:35
  557.4 233.4 %all-reduce.5.cloned.1.call-start = ((), (), s32[]{:S(2)}) async-start(), calls=%async_computation.2 | async-start | bytes 524288 | tf_op jit(solution)/shard_map/psum | solution.py:41
  704.6 2.3 copy-start
Sparse Core Ops, SparseCore 0:
  10.1 199.3 all-gather.5
  319.4 51.1 all-gather.7
  468.5 83.6 all-reduce.2
  557.5 50.8 all-gather.9
  707.0 83.7 all-reduce.4

commit v2 on v0

--- a/solution.py
+++ b/solution.py
@@ -16,7 +16,9 @@
     rank_cols = sketch_sign_flags.shape[3]
     group_count = outlier.shape[0]
     highest = lax.Precision.HIGHEST
-    weight_piece = lax.all_gather(key_value_weight, "seq", axis=0, tiled=True)
+    weight_piece = jnp.concatenate(
+        lax.all_to_all(jnp.stack([key_value_weight] * lax.axis_size("seq")), "seq", 0, 0), axis=0
+    )
     flat_piece = weight_piece.reshape(weight_piece.shape[0], head_count * kv_cols)
     projected_key_value = jnp.dot(hidden, flat_piece, precision=highest)
     projected_key_value = projected_key_value * row_scale[:, None]

time: 860 us -> 1300 us (1.51)
  waiting for transfers between devices: 536 us -> 960 us
    all_to_all x0 -> x1, waiting for transfers between devices: none -> 620 us  [shards(): lax.all_to_all(jnp.stack([key_value_weight] * lax.axis_size('seq')), 'seq...]
    all_gather x1 -> x0, waiting for transfers between devices: 201 us -> none  [shards(): weight_piece = lax.all_gather(key_value_weight, 'seq', axis=0, tiled=True)]
where the time goes in v2:
time: 1300 us
  waiting for transfers between devices  960 us (74%)
  other arithmetic  191 us (15%)
  matrix products  78.2 us (6%)
  local copies, waits for them, and re-layouts  52.3 us (4%)
  between operations  14 us (1%)
    all_to_all x1, waiting for transfers between devices, shards(): lax.all_to_all(jnp.stack([key_value_weight] * lax.axis_size('seq')), 'seq...  620 us
    psum x2, waiting for transfers between devices, shards(): gram_matrix = lax.psum(local_gram, 'seq')  174 us
    psum x2, waiting for transfers between devices, shards(): coefficient_rows = lax.psum(local_coef, 'seq')  166 us
    another operation x7, other arithmetic, shards(): lower_factor = jnp.linalg.cholesky(gram_matrix)  95.6 us
    another operation x5, other arithmetic, shards(): jax.scipy.linalg.solve_triangular(lower_factor, identity, lower=True)  81.7 us
    dot_general x1, matrix products, shards(): projected_key_value = jnp.dot(hidden, flat_piece, precision=highest)  60.5 us
    unnamed x11, local copies, waits for them, and re-layouts  29.4 us
  transfers between devices with their start and end apart: 5, of which 5 were waited for; matrix products, arithmetic and copies ran while one was open for 0% of the time, Pallas kernels for 0%

profile of v2, /device:TPU:0, one launch (start us, length us, event | category | flops | bytes accessed | tf_op | source)
XLA Modules:
  0.0 1302.5 jit_solution(14148888333844979701)
XLA Ops:
  7.2 12.3 stack.2
  19.5 7.3 all-to-all-start
  27.1 620.1 %all-to-all-done = f32[16,512,4,256]{3,2,1,0:T(4,128)} async-done(((f32[16,512,4,256]{3,2,1,0:T(4,128)}), f32[16,512,4,256]{3,2,1,0:T(4,128)}, u32[]{:S(2)}, u32[]{:S(2)}) %all-to-all-start) | async-done | bytes 33554464 | tf_op jit(solution)/shard_map/all_to_all | solution.py:20
  647.1 27.5 %copy.108 = f32[1024,8,4,256]{3,1,2,0:T(8,128)} copy(f32[1024,8,4,256]{3,2,1,0:T(4,128)} %bitcast.19) | data formatting | bytes 67108864
  674.7 60.5 %multiply_abs_fusion = (f32[512,1024]{1,0:T(8,128)}, f32[512,1024]{1,0:T(8,128)}) fusion(f32[512]{0:T(512)S(1)} %copy-done.3, f32[512,8192]{1,0:T(8,128)} %param.8, f32[8192,1024]{1,0:T(8,128)} %bitcast.59), kind=kOutput, calls=%fused_computation.3 | convolution fusion | flops 51541180416 | bytes 54528000 | tf_op jit(solution)/shard_map/dot_general | solution.py:23
  735.2 2.2 abs.7
  737.8 2.1 div.32
  740.0 1.9 copy.86
  741.9 1.8 copy.88
  743.7 8.9 fusion.1
  752.6 2.4 convolution_bitcast_fusion.1
  755.0 1.8 fusion.21
  756.9 90.1 %all-reduce.5.cloned.1.call-done = f32[4,2,64,64]{2,3,1,0:T(8,128)} async-done(((f32[4,2,64,64]{2,3,1,0:T(8,128)}), f32[4,2,64,64]{2,3,1,0:T(8,128)}) %all-reduce.5.cloned.1.call-update) | async-done | bytes 131088 | tf_op jit(solution)/shard_map/psum | solution.py:37
  847.0 1.1 copy.91
  848.1 1.7 fusion.9
  849.8 47.6 %custom-call.8 = f32[4,2,64,64]{3,2,1,0:T(8,128)S(1)} custom-call(f32[4,2,64,64]{3,2,1,0:T(8,128)} %fusion.9), custom_call_target="Cholesky" | custom-call | tf_op jit(solution)/shard_map/jit(cholesky)/cholesky | solution.py:38
  898.4 40.0 %custom-call.9 = f32[4,2,1,64,64]{3,4,2,1,0:T(8,128)S(1)} custom-call(f32[4,2,1,64,64]{4,3,2,1,0:T(8,128)} %select_bitcast_fusion.1), custom_call_target="InvertDiagBlocksLowerTriangular" | custom-call | tf_op jit(solution)/shard_map/jit(_solve_triangular)/vmap(vmap())/triangular_solve | solution.py:40
  939.1 1.0 convolution_bitcast_fusion.2
  940.1 2.2 fusion.22
  942.4 83.5 %all-reduce.7.cloned.1.call-done = f32[4,2,128,64]{2,3,1,0:T(8,128)} async-done(((f32[4,2,128,64]{2,3,1,0:T(8,128)}), f32[4,2,128,64]{2,3,1,0:T(8,128)}) %all-reduce.7.cloned.1.call-update) | async-done | bytes 262160 | tf_op jit(solution)/shard_map/psum | solution.py:43
  1025.8 3.3 convolution_bitcast_fusion
  1029.2 1.8 fusion.23
  1031.0 83.5 %all-reduce.9.cloned.1.call-done = f32[4,2,64,64]{2,3,1,0:T(8,128)} async-done(((f32[4,2,64,64]{2,3,1,0:T(8,128)}), f32[4,2,64,64]{2,3,1,0:T(8,128)}) %all-reduce.9.cloned.1.call-update) | async-done | bytes 131088 | tf_op jit(solution)/shard_map/psum | solution.py:37
  1114.5 1.1 copy.96
  1115.6 1.7 fusion.6
  1117.3 47.6 %custom-call.10 = f32[4,2,64,64]{3,2,1,0:T(8,128)S(1)} custom-call(f32[4,2,64,64]{3,2,1,0:T(8,128)} %fusion.6), custom_call_target="Cholesky" | custom-call | tf_op jit(solution)/shard_map/jit(cholesky)/cholesky | solution.py:38
  1165.9 40.0 %custom-call.11 = f32[4,2,1,64,64]{3,4,2,1,0:T(8,128)S(1)} custom-call(f32[4,2,1,64,64]{4,3,2,1,0:T(8,128)} %select_bitcast_fusion), custom_call_target="InvertDiagBlocksLowerTriangular" | custom-call | tf_op jit(solution)/shard_map/jit(_solve_triangular)/vmap(vmap())/triangular_solve | solution.py:40
  1206.6 1.8 multiply_convert_fusion
  1208.4 2.2 fusion.2
  1210.6 1.0 copy.100
  1211.6 82.5 %all-reduce.11.cloned.1.call-done = f32[4,2,128,64]{2,3,1,0:T(8,128)} async-done(((f32[4,2,128,64]{2,3,1,0:T(8,128)}), f32[4,2,128,64]{2,3,1,0:T(8,128)}) %all-reduce.11.cloned.1.call-update) | async-done | bytes 262160 | tf_op jit(solution)/shard_map/psum | solution.py:43
  1294.2 1.0 broadcast_multiply_fusion
  (34 shorter events, 4.9 us)
Async XLA Ops:
  19.5 7.4 copy-start.2
  19.5 627.6 %all-to-all-start = ((f32[16,512,4,256]{3,2,1,0:T(4,128)}), f32[16,512,4,256]{3,2,1,0:T(4,128)}, u32[]{:S(2)}, u32[]{:S(2)}) async-start(f32[16,512,4,256]{3,2,1,0:T(4,128)} %stack.2), calls=%async_computation | async-start | bytes 67108864 | tf_op jit(solution)/shard_map/all_to_all | solution.py:20
  26.8 820.2 %all-reduce.5.cloned.1.call-start = ((), (), s32[]{:S(2)}) async-start(), calls=%async_computation.1 | async-start | bytes 524288 | tf_op jit(solution)/shard_map/psum | solution.py:37
  647.1 27.5 %copy-start.3 = (f32[512]{0:T(512)S(1)}, f32[512]{0:T(512)}, u32[]{:S(2)}) copy-start(f32[512]{0:T(512)} %param.9) | copy-start | bytes 6148
  743.7 8.9 copy-start.1
  756.8 269.0 %all-reduce.7.cloned.1.call-start = ((), (), s32[]{:S(2)}) async-start(), calls=%async_computation.2 | async-start | bytes 524288 | tf_op jit(solution)/shard_map/psum | solution.py:43
  942.3 172.2 %all-reduce.9.cloned.1.call-start = ((), (), s32[]{:S(2)}) async-start(), calls=%async_computation.3 | async-start | bytes 524288 | tf_op jit(solution)/shard_map/psum | solution.py:37
  1031.0 263.2 %all-reduce.11.cloned.1.call-start = ((), (), s32[]{:S(2)}) async-start(), calls=%async_computation.4 | async-start | bytes 524288 | tf_op jit(solution)/shard_map/psum | solution.py:43
  1208.4 2.3 copy-start
Sparse Core Ops, SparseCore 0:
  757.0 90.0 all-reduce.4
  942.4 83.3 all-reduce.6
  1031.1 83.3 all-reduce.8
  1210.7 83.3 all-reduce.10
